TPU v7x, 256 devices: a whole 4x4x8 slice. The times are simulated.
256 devices in a mesh: ep: 64 (over z, x, y_hi), tp: 4 (over y_lo, core).
Axes of the slice: x: 4, y: 4 (y_hi: 2, y_lo: 2; y = y_hi * 2 + y_lo), z: 8, core: 2. Of those that a mesh axis runs over, the one named last changes fastest.
Arguments:
- context: bfloat16 [8192, 4096], P('ep', 'tp'), may hold values from -6 to 6
- wo_proj: bfloat16 [4096, 4096], P('tp'), may hold values from -0.09375 to 0.09375
- residual: bfloat16 [8192, 4096], P(('ep', 'tp')), may hold values from -16 to 16
- norm_gain: bfloat16 [4096], replicated, may hold values from 0.25 to 1.75
- expert_ids: int32 [8192, 8], P(('ep', 'tp')), may hold values from 0 to 63, all different within a row; in each aligned block of 32 rows (0 to 31, 32 to 63, ...) at most 8 rows name the same one
- route_weights: float32 [8192, 8], P(('ep', 'tp')), may hold values from 0.1 to 1
- w_gate_up: bfloat16 [64, 2, 768, 4096], P('ep', None, 'tp'), may hold values from -0.09375 to 0.09375
- w_down: bfloat16 [64, 768, 4096], P('ep', 'tp'), may hold values from -0.21875 to 0.21875
Outputs:
- layer_out: bfloat16 [8192, 4096], P(('ep', 'tp'))
Inputs may be any that keep to these rules, and one draw needn't show every extreme that they name: `expert_ids`: within the routes of one device's 32 tokens no expert is named more than 8 times, a bound that some block reaches; a token names 8 different experts.
All inputs are finite; a program needn't handle non-finite values.
Results may differ from a plain program's by a relative error of at most 0.0085.
Values may be sent and summed in bfloat16 or wider, within the bound.
A program may use at most 128 MiB of HBM per device.

v0:
```python
import jax
import jax.numpy as jnp
from jax import lax
from jax.sharding import PartitionSpec as P


def local(context, wo_proj, residual, norm_gain, expert_ids, route_weights, w_gate_up, w_down):
    quarter_rows, model_width = residual.shape
    top_count = expert_ids.shape[1]
    exp_local = w_gate_up.shape[0]
    ep_size = lax.axis_size("ep")
    experts = exp_local * ep_size
    capacity = max(2, min(quarter_rows, 2 * quarter_rows * top_count // experts))
    attn = lax.psum_scatter(
        jnp.dot(context, wo_proj, preferred_element_type=jnp.float32),
        "tp",
        scatter_dimension=0,
        tiled=True,
    )
    hidden = residual.astype(jnp.float32) + attn
    inverse_rms = lax.rsqrt(jnp.mean(hidden * hidden, axis=1, keepdims=True) + 1e-06)
    normed = (hidden * inverse_rms * norm_gain.astype(jnp.float32)).astype(jnp.bfloat16)
    flat_ids = expert_ids.reshape(-1)
    onehot = (flat_ids[:, None] == jnp.arange(experts, dtype=jnp.int32)[None, :]).astype(jnp.int32)
    before = jnp.cumsum(onehot, axis=0, dtype=jnp.int32) - onehot
    position = jnp.sum(before * onehot, axis=1, dtype=jnp.int32)
    slot_ids = flat_ids * capacity + position
    slot_range = jnp.arange(experts * capacity, dtype=jnp.int32)
    selected = slot_range[:, None] == slot_ids[None, :]
    placement = jnp.any(
        selected.reshape(experts * capacity, quarter_rows, top_count), axis=2
    ).astype(jnp.bfloat16)
    send_rows = jnp.dot(placement, normed, preferred_element_type=jnp.float32).astype(jnp.bfloat16)
    send_rows = send_rows.reshape(ep_size, exp_local * capacity, model_width)
    received = lax.all_to_all(send_rows, "ep", split_axis=0, concat_axis=0, tiled=True)
    received = received.reshape(ep_size, exp_local, capacity, model_width)
    piece = lax.all_gather(received[None], "tp", axis=0, tiled=True)
    gate = jnp.einsum(
        "nsjcd,jfd->nsjcf", piece, w_gate_up[:, 0], preferred_element_type=jnp.float32
    )
    up_proj = jnp.einsum(
        "nsjcd,jfd->nsjcf", piece, w_gate_up[:, 1], preferred_element_type=jnp.float32
    )
    activated = (jax.nn.silu(gate) * up_proj).astype(jnp.bfloat16)
    partials = jnp.einsum("nsjcf,jfd->nsjcd", activated, w_down, preferred_element_type=jnp.float32)
    combined = lax.psum_scatter(
        partials.astype(jnp.bfloat16), "tp", scatter_dimension=0, tiled=True
    ).astype(jnp.float32)
    expert_out = combined[0].astype(jnp.bfloat16)
    returned = lax.all_to_all(
        expert_out.reshape(ep_size, exp_local * capacity, model_width),
        "ep",
        split_axis=0,
        concat_axis=0,
        tiled=True,
    )
    returned = returned.reshape(experts * capacity, model_width)
    token_slots = slot_ids.reshape(quarter_rows, top_count)
    mixture = jnp.zeros((quarter_rows, model_width), jnp.float32)
    for choice_index in range(top_count):
        picker = (slot_range[None, :] == token_slots[:, choice_index][:, None]).astype(jnp.bfloat16)
        picked = jnp.dot(picker, returned, preferred_element_type=jnp.float32)
        mixture = mixture + route_weights[:, choice_index : choice_index + 1] * picked
    return (hidden + mixture).astype(jnp.bfloat16)


def solution(mesh):
    in_specs = (
        P("ep", "tp"),
        P("tp", None),
        P(("ep", "tp"), None),
        P(),
        P(("ep", "tp"), None),
        P(("ep", "tp"), None),
        P("ep", None, "tp", None),
        P("ep", "tp", None),
    )
    out_specs = P(("ep", "tp"), None)
    return jax.shard_map(local, mesh=mesh, in_specs=in_specs, out_specs=out_specs, check_vma=False)
```

profile of v0, /device:TPU:32, one launch (start us, length us, event | category | flops | bytes accessed | tf_op | source)
XLA Modules:
  0.0 636.2 jit_solution(903657910014447604)
XLA Ops:
  6.5 0.0 reduce-scatter.3.cloned.1.call-start
  6.6 6.2 fusion.50
  12.8 0.0 all-gather.3.cloned.1.call-start
  12.9 0.1 copy.22
  12.9 0.1 eq.164
  13.0 0.1 eq.160
  13.2 0.6 reduce-window.6
  13.8 0.2 slice_reduce_fusion
  14.0 0.1 fusion.39
  14.1 0.1 reduce_sum.21
  14.2 0.2 fusion.34
  14.5 31.8 %reduce-scatter.3.cloned.1.call-done = f32[32,4096]{1,0:T(8,128)} async-done(((f32[128,4096]{1,0:T(8,128)}), f32[32,4096]{1,0:T(8,128)}) %reduce-scatter.3.cloned.1.call-update) | async-done | bytes 524304 | tf_op jit(solution)/shard_map/reduce_scatter | solution.py:14
  46.2 1.2 multiply_reduce_fusion
  47.5 2.4 fusion
  49.8 109.7 %all_to_all.10 = bf16[64,8,4096]{2,1,0:T(8,128)(2,1)} all-to-all(bf16[64,8,4096]{2,1,0:T(8,128)(2,1)S(1)} %fusion), channel_id=1, replica_groups=mesh['ep'=64,'tp'=4] {'ep'}, dimensions={0} | all-to-all | bytes 8388608 | tf_op jit(solution)/shard_map/all_to_all | solution.py:35
  159.5 0.0 all-gather.3.cloned.1.call-update
  159.5 0.2 reduce-scatter.5.cloned.1.call-start
  159.8 147.1 %all-gather.3.cloned.1.call-done = bf16[256,8,4096]{2,1,0:T(8,128)(2,1)} async-done(((bf16[64,8,4096]{2,1,0:T(8,128)(2,1)}), bf16[256,8,4096]{2,1,0:T(8,128)(2,1)}) %all-gather.3.cloned.1.call-update) | async-done | bytes 16777232 | tf_op jit(solution)/shard_map/all_gather | solution.py:37
  306.9 12.2 %fusion.23 = f32[4,64,8,192]{3,2,1,0:T(8,128)} fusion(bf16[4,64,8,4096]{3,2,1,0:T(8,128)(2,1)} %bitcast.130, bf16[1,2,192,4096]{3,2,1,0:T(8,128)(2,1)} %param.14), kind=kOutput, calls=%fused_computation.36 | convolution fusion | flops 3221225472 | bytes 19922944 | tf_op jit(solution)/shard_map/nsjcd,jfd->nsjcf/dot_general | solution.py:41
  319.0 23.8 %convert_bitcast_fusion = bf16[4,64,1,8,4096]{4,3,1,0,2:T(8,128)(2,1)} fusion(bf16[1,192,4096]{2,1,0:T(8,128)(2,1)S(1)} %copy-done, f32[4,64,8,192]{3,2,1,0:T(8,128)} %fusion.23, bf16[4,64,8,4096]{3,2,1,0:T(8,128)(2,1)} %bitcast.131, bf16[1,2,192,4096]{3,2,1,0:T(8,128)(2,1)} %param.14), kind=kOutput, calls=%fused_computation | convolution fusion | flops 6453198848 | bytes 38797312 | tf_op jit(solution)/shard_map/nsjcf,jfd->nsjcd/dot_general | solution.py:45
  342.9 151.7 %reduce-scatter.5.cloned.1.call-done = bf16[1,64,1,8,4096]{4,3,1,0,2:T(8,128)(2,1)} async-done(((bf16[4,64,1,8,4096]{4,3,1,0,2:T(8,128)(2,1)}), bf16[1,64,1,8,4096]{4,3,1,0,2:T(8,128)(2,1)}) %reduce-scatter.5.cloned.1.call-update) | async-done | bytes 4194320 | tf_op jit(solution)/shard_map/reduce_scatter | solution.py:46
  494.6 12.9 %all-to-all-start.1 = ((bf16[64,8,4096]{2,1,0:T(8,128)(2,1)}), bf16[64,8,4096]{2,1,0:T(8,128)(2,1)}, u32[]{:S(2)}, u32[]{:S(2)}) async-start(bf16[64,8,4096]{2,1,0:T(8,128)(2,1)} %bitcast.129), calls=%async_computation.3 | async-start | bytes 8388608 | tf_op jit(solution)/shard_map/all_to_all | solution.py:50
  507.5 0.3 slice_reduce_fusion.1
  507.8 96.5 %all-to-all-done.1 = bf16[64,8,4096]{2,1,0:T(8,128)(2,1)} async-done(((bf16[64,8,4096]{2,1,0:T(8,128)(2,1)}), bf16[64,8,4096]{2,1,0:T(8,128)(2,1)}, u32[]{:S(2)}, u32[]{:S(2)}) %all-to-all-start.1) | async-done | bytes 4194336 | tf_op jit(solution)/shard_map/all_to_all | solution.py:50
  604.3 3.0 convolution_multiply_fusion.7
  607.3 3.0 fusion.8
  610.4 3.0 fusion.7
  613.5 3.0 fusion.6
  616.5 3.0 fusion.5
  619.6 3.1 fusion.4
  622.7 3.2 fusion.3
  625.9 3.8 fusion.9
  (23 shorter events, 0.1 us)
Async XLA Ops:
  6.5 312.5 %copy-start = (bf16[1,192,4096]{2,1,0:T(8,128)(2,1)S(1)}, bf16[1,192,4096]{2,1,0:T(8,128)(2,1)}, u32[]{:S(2)}) copy-start(bf16[1,192,4096]{2,1,0:T(8,128)(2,1)} %param.15) | copy-start | bytes 4718596
  6.5 6.3 copy-start.5
  6.5 6.6 %copy-start.4 = (bf16[4096]{0:T(1024)(128)(2,1)S(1)}, bf16[4096]{0:T(1024)(128)(2,1)}, u32[]{:S(2)}) copy-start(bf16[4096]{0:T(1024)(128)(2,1)} %param.11) | copy-start | bytes 24580
  6.5 39.7 %copy-start.3 = (bf16[32,4096]{1,0:T(8,128)(2,1)S(1)}, bf16[32,4096]{1,0:T(8,128)(2,1)}, u32[]{:S(2)}) copy-start(bf16[32,4096]{1,0:T(8,128)(2,1)} %param.10) | copy-start | bytes 786436
  6.5 39.7 %reduce-scatter.3.cloned.1.call-start = ((), (), s32[]{:S(2)}) async-start(), calls=%async_computation.4 | async-start | bytes 2621440 | tf_op jit(solution)/shard_map/reduce_scatter | solution.py:14
  12.8 294.0 %all-gather.3.cloned.1.call-start = ((), (), s32[]{:S(2)}) async-start(), calls=%async_computation.6 | async-start | bytes 20971520 | tf_op jit(solution)/shard_map/all_gather | solution.py:37
  159.5 335.0 %reduce-scatter.5.cloned.1.call-start = ((), (), s32[]{:S(2)}) async-start(), calls=%async_computation.5 | async-start | bytes 20971520 | tf_op jit(solution)/shard_map/reduce_scatter | solution.py:46
  494.6 13.3 %copy-start.6 = (f32[32,8]{0,1:T(8,128)S(1)}, f32[32,8]{0,1:T(8,128)}, u32[]{:S(2)}) copy-start(f32[32,8]{0,1:T(8,128)} %param.13) | copy-start | bytes 3076
  494.6 109.7 %all-to-all-start.1 = ((bf16[64,8,4096]{2,1,0:T(8,128)(2,1)}), bf16[64,8,4096]{2,1,0:T(8,128)(2,1)}, u32[]{:S(2)}, u32[]{:S(2)}) async-start(bf16[64,8,4096]{2,1,0:T(8,128)(2,1)} %bitcast.129), calls=%async_computation.3 | async-start | bytes 8388608 | tf_op jit(solution)/shard_map/all_to_all | solution.py:50
  619.6 6.3 copy-start.2
  622.7 7.0 %copy-start.1 = (bf16[1,192,4096]{2,1,0:T(8,128)(2,1)S(1)}, bf16[1,192,4096]{2,1,0:T(8,128)(2,1)}, u32[]{:S(2)}) copy-start(bf16[1,192,4096]{2,1,0:T(8,128)(2,1)} %param.15) | copy-start | bytes 4718596
Sparse Core Ops, SparseCore 0:
  12.9 33.2 reduce-scatter.2
  159.7 147.1 all-gather.2
  343.0 151.5 reduce-scatter.4
where the time goes:
time: 637 us; the launch traced here: 636 us
  waiting for transfers between devices  427 us (67%)
  blocking collectives  110 us (17%)
  matrix products  69.8 us (11%)
  between operations  13.3 us (2%)
  starting transfers between devices  13.2 us (2%)
    reduce_scatter x1, waiting for transfers between devices, local(): lax.psum_scatter(partials.astype(jnp.bfloat16), 'tp', scatter_dimension=0...  152 us
    all_gather x1, waiting for transfers between devices, local(): piece = lax.all_gather(received[None], 'tp', axis=0, tiled=True)  147 us
    all_to_all x1, blocking collectives, local(): lax.all_to_all(send_rows, 'ep', split_axis=0, concat_axis=0, tiled=True)  110 us
    all_to_all x1, waiting for transfers between devices, local(): lax.all_to_all(expert_out.reshape(ep_size, exp_local * capacity, model_wi...  96.5 us
    reduce_scatter x1, waiting for transfers between devices, local(): lax.psum_scatter(jnp.dot(context, wo_proj, preferred_element_type=jnp.flo...  31.8 us
    dot_general x8, matrix products, local(): picked = jnp.dot(picker, returned, preferred_element_type=jnp.float32)  25.3 us
    dot_general x1, matrix products, local(): jnp.einsum('nsjcf,jfd->nsjcd', activated, w_down, preferred_element_type=...  23.8 us
    all_to_all x1, starting transfers between devices, local(): lax.all_to_all(expert_out.reshape(ep_size, exp_local * capacity, model_wi...  12.9 us
  transfers between devices with their start and end apart: 4, of which 4 were waited for; matrix products, arithmetic and copies ran while one was open for 0% of the time, Pallas kernels for 0%

commit v1 on v0

--- a/solution.py
+++ b/solution.py
@@ -34,7 +34,14 @@
     send_rows = send_rows.reshape(ep_size, exp_local * capacity, model_width)
     received = lax.all_to_all(send_rows, "ep", split_axis=0, concat_axis=0, tiled=True)
     received = received.reshape(ep_size, exp_local, capacity, model_width)
-    piece = lax.all_gather(received[None], "tp", axis=0, tiled=True)
+
+    def streams_turn(local_array, device_axis):
+        seen_now = lax.axis_size(device_axis)
+        all_rows = jnp.stack([local_array] * seen_now)
+        piece_now = lax.all_to_all(all_rows, axis_name=device_axis, split_axis=0, concat_axis=0)
+        return jnp.concatenate(piece_now, axis=0)
+
+    piece = streams_turn(received[None], device_axis="tp")
     gate = jnp.einsum(
         "nsjcd,jfd->nsjcf", piece, w_gate_up[:, 0], preferred_element_type=jnp.float32
     )

time: 637 us -> 672 us (1.055)
  blocking collectives: 110 us -> 297 us
  waiting for transfers between devices: 427 us -> 273 us
    all_to_all x0 -> x1, blocking collectives: none -> 187 us  [streams_turn(): lax.all_to_all(all_rows, axis_name=device_axis, split_axis=0, concat_axis=0)]
    all_gather x1 -> x0, waiting for transfers between devices: 147 us -> none  [local(): piece = lax.all_gather(received[None], 'tp', axis=0, tiled=True)]
    reduce_scatter x1, waiting for transfers between devices: 152 us -> 144 us  [local(): lax.psum_scatter(partials.astype(jnp.bfloat16), 'tp', scatter_dimension=0...]
  transfers between devices with their start and end apart: 4 -> 3, of which waited for: 4 -> 3; matrix products, arithmetic and copies ran while one was open for 0% -> 0% of each run, Pallas kernels for 0% -> 0%
where the time goes in v1:
time: 672 us; the launch traced here: 671 us
  blocking collectives  297 us (44%)
  waiting for transfers between devices  273 us (41%)
  matrix products  69.8 us (10%)
  between operations  13.6 us (2%)
  starting transfers between devices  13 us (2%)
    all_to_all x1, blocking collectives, streams_turn(): lax.all_to_all(all_rows, axis_name=device_axis, split_axis=0, concat_axis=0)  187 us
    reduce_scatter x1, waiting for transfers between devices, local(): lax.psum_scatter(partials.astype(jnp.bfloat16), 'tp', scatter_dimension=0...  144 us
    all_to_all x1, blocking collectives, local(): lax.all_to_all(send_rows, 'ep', split_axis=0, concat_axis=0, tiled=True)  110 us
    all_to_all x1, waiting for transfers between devices, local(): lax.all_to_all(expert_out.reshape(ep_size, exp_local * capacity, model_wi...  96.5 us
    reduce_scatter x1, waiting for transfers between devices, local(): lax.psum_scatter(jnp.dot(context, wo_proj, preferred_element_type=jnp.flo...  31.8 us
    dot_general x8, matrix products, local(): picked = jnp.dot(picker, returned, preferred_element_type=jnp.float32)  25.2 us
    dot_general x1, matrix products, local(): jnp.einsum('nsjcf,jfd->nsjcd', activated, w_down, preferred_element_type=...  23.8 us
  transfers between devices with their start and end apart: 3, of which 3 were waited for; matrix products, arithmetic and copies ran while one was open for 0% of the time, Pallas kernels for 0%

profile of v1, /device:TPU:32, one launch (start us, length us, event | category | flops | bytes accessed | tf_op | source)
XLA Modules:
  0.0 671.0 jit_solution(5180338689358919531)
XLA Ops:
  6.5 0.0 reduce-scatter.3.cloned.1.call-start
  6.6 6.2 fusion.59
  12.8 0.0 reduce-scatter.5.cloned.1.call-start
  12.9 0.1 copy.22
  12.9 0.1 eq.164
  13.0 0.1 eq.160
  13.2 0.6 reduce-window.6
  13.8 0.2 slice_reduce_fusion
  14.0 0.1 fusion.48
  14.1 0.1 reduce_sum.21
  14.2 0.2 fusion.43
  14.5 31.8 %reduce-scatter.3.cloned.1.call-done = f32[32,4096]{1,0:T(8,128)} async-done(((f32[128,4096]{1,0:T(8,128)}), f32[32,4096]{1,0:T(8,128)}) %reduce-scatter.3.cloned.1.call-update) | async-done | bytes 524304 | tf_op jit(solution)/shard_map/reduce_scatter | solution.py:14
  46.2 1.2 multiply_reduce_fusion
  47.5 2.4 fusion.4
  49.8 109.6 %all_to_all.15 = bf16[64,8,4096]{2,1,0:T(8,128)(2,1)S(1)} all-to-all(bf16[64,8,4096]{2,1,0:T(8,128)(2,1)S(1)} %fusion.4), channel_id=1, replica_groups=mesh['ep'=64,'tp'=4] {'ep'}, dimensions={0} | all-to-all | bytes 8388608 | tf_op jit(solution)/shard_map/all_to_all | solution.py:35
  159.4 2.1 stack.3
  161.5 187.3 %all_to_all.16 = bf16[4,1,64,1,8,4096]{5,4,2,3,1,0:T(8,128)(2,1)} all-to-all(bf16[4,1,64,1,8,4096]{5,4,2,3,1,0:T(8,128)(2,1)S(1)} %stack.3), channel_id=1, replica_groups=mesh['ep'=64,'tp'=4] {'tp'}, dimensions={0} | all-to-all | bytes 33554432 | tf_op jit(solution)/shard_map/all_to_all | solution.py:41
  348.8 12.2 %fusion = f32[4,64,8,192]{3,2,1,0:T(8,128)} fusion(bf16[4,1,64,1,8,4096]{5,4,2,3,1,0:T(8,128)(2,1)} %all_to_all.16, bf16[1,2,192,4096]{3,2,1,0:T(8,128)(2,1)} %param.14), kind=kOutput, calls=%fused_computation | convolution fusion | flops 3221225472 | bytes 19922944 | tf_op jit(solution)/shard_map/nsjcd,jfd->nsjcf/dot_general | solution.py:48
  361.0 23.8 %convert_bitcast_fusion = bf16[4,64,1,8,4096]{4,3,1,0,2:T(8,128)(2,1)} fusion(bf16[1,192,4096]{2,1,0:T(8,128)(2,1)S(1)} %copy-done, f32[4,64,8,192]{3,2,1,0:T(8,128)} %fusion, bf16[1,2,192,4096]{3,2,1,0:T(8,128)(2,1)} %param.14, bf16[4,1,64,1,8,4096]{5,4,2,3,1,0:T(8,128)(2,1)} %all_to_all.16), kind=kOutput, calls=%fused_computation.4 | convolution fusion | flops 6453198848 | bytes 38797312 | tf_op jit(solution)/shard_map/nsjcf,jfd->nsjcd/dot_general | solution.py:52
  384.8 0.0 reduce-scatter.5.cloned.1.call-update
  384.9 144.3 %reduce-scatter.5.cloned.1.call-done = bf16[1,64,1,8,4096]{4,3,1,0,2:T(8,128)(2,1)} async-done(((bf16[4,64,1,8,4096]{4,3,1,0,2:T(8,128)(2,1)}), bf16[1,64,1,8,4096]{4,3,1,0,2:T(8,128)(2,1)}) %reduce-scatter.5.cloned.1.call-update) | async-done | bytes 4194320 | tf_op jit(solution)/shard_map/reduce_scatter | solution.py:53
  529.2 12.9 %all-to-all-start.2 = ((bf16[64,8,4096]{2,1,0:T(8,128)(2,1)}), bf16[64,8,4096]{2,1,0:T(8,128)(2,1)}, u32[]{:S(2)}, u32[]{:S(2)}) async-start(bf16[64,8,4096]{2,1,0:T(8,128)(2,1)} %bitcast.137), calls=%async_computation.4 | async-start | bytes 8388608 | tf_op jit(solution)/shard_map/all_to_all | solution.py:57
  542.1 0.3 slice_reduce_fusion.1
  542.4 96.5 %all-to-all-done.2 = bf16[64,8,4096]{2,1,0:T(8,128)(2,1)} async-done(((bf16[64,8,4096]{2,1,0:T(8,128)(2,1)}), bf16[64,8,4096]{2,1,0:T(8,128)(2,1)}, u32[]{:S(2)}, u32[]{:S(2)}) %all-to-all-start.2) | async-done | bytes 4194336 | tf_op jit(solution)/shard_map/all_to_all | solution.py:57
  638.9 3.0 convolution_multiply_fusion.7
  642.0 3.0 fusion.12
  645.0 3.0 fusion.11
  648.0 3.0 fusion.10
  651.1 3.0 fusion.9
  654.1 3.1 fusion.8
  657.2 3.2 fusion.7
  660.4 3.8 fusion.13
  (22 shorter events, 0.1 us)
Async XLA Ops:
  6.5 354.5 %copy-start = (bf16[1,192,4096]{2,1,0:T(8,128)(2,1)S(1)}, bf16[1,192,4096]{2,1,0:T(8,128)(2,1)}, u32[]{:S(2)}) copy-start(bf16[1,192,4096]{2,1,0:T(8,128)(2,1)} %param.15) | copy-start | bytes 4718596
  6.5 6.3 copy-start.5
  6.5 6.6 copy-start.4
  6.5 39.7 %copy-start.3 = (bf16[32,4096]{1,0:T(8,128)(2,1)S(1)}, bf16[32,4096]{1,0:T(8,128)(2,1)}, u32[]{:S(2)}) copy-start(bf16[32,4096]{1,0:T(8,128)(2,1)} %param.10) | copy-start | bytes 786436
  6.5 39.7 %reduce-scatter.3.cloned.1.call-start = ((), (), s32[]{:S(2)}) async-start(), calls=%async_computation.5 | async-start | bytes 2621440 | tf_op jit(solution)/shard_map/reduce_scatter | solution.py:14
  12.8 516.4 %reduce-scatter.5.cloned.1.call-start = ((), (), s32[]{:S(2)}) async-start(), calls=%async_computation.6 | async-start | bytes 20971520 | tf_op jit(solution)/shard_map/reduce_scatter | solution.py:53
  529.2 13.3 %copy-start.6 = (f32[32,8]{0,1:T(8,128)S(1)}, f32[32,8]{0,1:T(8,128)}, u32[]{:S(2)}) copy-start(f32[32,8]{0,1:T(8,128)} %param.13) | copy-start | bytes 3076
  529.2 109.7 %all-to-all-start.2 = ((bf16[64,8,4096]{2,1,0:T(8,128)(2,1)}), bf16[64,8,4096]{2,1,0:T(8,128)(2,1)}, u32[]{:S(2)}, u32[]{:S(2)}) async-start(bf16[64,8,4096]{2,1,0:T(8,128)(2,1)} %bitcast.137), calls=%async_computation.4 | async-start | bytes 8388608 | tf_op jit(solution)/shard_map/all_to_all | solution.py:57
  654.1 6.3 copy-start.2
  657.2 7.0 %copy-start.1 = (bf16[1,192,4096]{2,1,0:T(8,128)(2,1)S(1)}, bf16[1,192,4096]{2,1,0:T(8,128)(2,1)}, u32[]{:S(2)}) copy-start(bf16[1,192,4096]{2,1,0:T(8,128)(2,1)} %param.15) | copy-start | bytes 4718596
Sparse Core Ops, SparseCore 0:
  12.9 33.2 reduce-scatter.2
  385.0 144.1 reduce-scatter.4
